TPU v7x, 256 devices: a whole 4x4x8 slice. The times are simulated.
256 devices in a mesh: seq: 32 (over y, x, core), tensor: 8 (over z).
Axes of the slice: x: 4, y: 4, z: 8, core: 2. Of those that a mesh axis runs over, the one named last changes fastest.
Arguments:
- queries: bfloat16 [4096, 8192], P('seq', 'tensor'), may hold values from -6 to 6
- key_vectors: bfloat16 [4096, 8192], P('seq', 'tensor'), may hold values from -6 to 6
- value_rows: bfloat16 [4096, 8192], P('seq', 'tensor'), may hold values from -6 to 6
- gate_logits: bfloat16 [4096, 8192], P('seq', 'tensor'), may hold values from -6 to 6
- log_decay: float32 [4096, 64], P('seq', 'tensor'), may hold values from -0.73 to 0, as said below
- initial_state: float32 [64, 128, 128], P('tensor'), may hold values from -192 to 192
- norm_gain: float32 [8192], P('tensor'), may hold values from 0.25 to 1.75
- out_weight: bfloat16 [8192, 6144], P('tensor', 'seq'), may hold values from -0.0625 to 0.0625
Outputs:
- mixed: float32 [4096, 6144], P('seq', 'tensor')
Inputs may be any that keep to these rules, and one draw needn't show every extreme that they name: `log_decay`: every entry is negative.
All inputs are finite; a program needn't handle non-finite values.
Results may differ from a plain program's by a relative error of at most 0.0075.
Values may be sent and summed in bfloat16 or wider, within the bound.
No kernel may reach another device: no remote copies, remote signals or barrier semaphores. Data moves between devices by JAX's collectives and lax.ppermute only.
A program may use at most 128 MiB of HBM per device.

v0:
```python
import jax
import jax.numpy as jnp
from jax import lax
from jax.sharding import PartitionSpec as P

HIGH = lax.Precision.HIGHEST


def entering(array, axis, combine, identity):
    length, mine = (lax.axis_size(axis), lax.axis_index(axis))
    everything = jax.tree.map(lambda part: lax.all_gather(part, axis), array)
    start = jax.tree.map(
        lambda part, zero: jnp.broadcast_to(jnp.asarray(zero, part.dtype), part.shape),
        array,
        identity,
    )

    def hop(k, before):
        reached = k < mine
        new = combine(before, jax.tree.map(lambda part: part[k], everything))
        return jax.tree.map(lambda a, b: jnp.where(reached, a, b), new, before)

    return lax.fori_loop(0, length, hop, start)


def block_step(state, pieces):
    queries_b, keys_b, values_b, decay_b = pieces
    cumulative_memory = jnp.cumsum(decay_b, axis=0)
    total = cumulative_memory[-1]
    carried = jnp.exp(cumulative_memory)[:, :, None] * jnp.einsum(
        "thd,hde->the", queries_b.astype(jnp.float32), state, precision=HIGH
    )
    scores = jnp.einsum("thd,shd->hts", queries_b, keys_b, preferred_element_type=jnp.float32)
    length = cumulative_memory.shape[0]
    lower = jnp.tril(jnp.ones((length, length), dtype=bool))[None]
    spread = cumulative_memory.T[:, :, None] - cumulative_memory.T[:, None, :]
    weights = jnp.where(lower, jnp.exp(jnp.where(lower, spread, 0.0)), 0.0)
    mixes = (scores * weights).astype(jnp.bfloat16)
    local = jnp.einsum("hts,she->the", mixes, values_b, preferred_element_type=jnp.float32)
    scaled = keys_b.astype(jnp.float32) * jnp.exp(total[None, :] - cumulative_memory)[:, :, None]
    new_state = jnp.exp(total)[:, None, None] * state + jnp.einsum(
        "shd,she->hde", scaled, values_b.astype(jnp.float32), precision=HIGH
    )
    return (new_state, carried + local)


def normalize(attended, norm_gain, gate_logits):
    mean_square = jnp.mean(attended * attended, axis=-1, keepdims=True)
    normalized_output = attended * lax.rsqrt(mean_square + 1e-05)
    flat = normalized_output.reshape(attended.shape[0], -1)
    gated = flat * norm_gain[None, :] * jax.nn.sigmoid(gate_logits.astype(jnp.float32))
    return gated.astype(jnp.bfloat16)


def chain_link(earlier, later):
    return (earlier[0] * later[0], later[0][:, None, None] * earlier[1] + later[1])


def pack(rates, state):
    heads = state.shape[0]
    flat = state.reshape(heads, -1)
    lanes = jnp.broadcast_to(rates[:, None], (heads, 128))
    return jnp.concatenate([flat, lanes], axis=1)


def link_packed(earlier, later):
    width = later.shape[1] - 128
    later_rate = later[:, width : width + 1]
    state = later_rate * earlier[:, :width] + later[:, :width]
    rate = earlier[:, width:] * later[:, width:]
    return jnp.concatenate([state, rate], axis=1)


def carried_in(rates, state, initial_state):
    length, mine = (lax.axis_size("seq"), lax.axis_index("seq"))
    own = pack(rates, state)
    shifted = lax.ppermute(own, "seq", [(i, i + 1) for i in range(length - 1)])
    first = pack(jnp.ones_like(rates), initial_state)
    current = jnp.where(mine == 0, first, shifted)
    step = 1
    while step < length:
        earlier = lax.ppermute(current, "seq", [(i, i + step) for i in range(length - step)])
        current = jnp.where(mine >= step, link_packed(earlier, current), current)
        step *= 2
    width = current.shape[1] - 128
    return current[:, :width].reshape(state.shape)


def per_device(
    queries, key_vectors, value_rows, gate_logits, log_decay, initial_state, norm_gain, out_weight
):
    rows_here = queries.shape[0]
    head_count = log_decay.shape[1]
    head_dim = initial_state.shape[1]
    block_len = min(512, rows_here)
    block_count = rows_here // block_len

    def shaped(array):
        return array.reshape(block_count, block_len, head_count, head_dim)

    zero_state = jnp.zeros((head_count, head_dim, head_dim), jnp.float32)
    decay_blocks = log_decay.reshape(block_count, block_len, head_count)
    device_state, outputs = lax.scan(
        block_step,
        zero_state,
        (shaped(queries), shaped(key_vectors), shaped(value_rows), decay_blocks),
    )
    local_out = outputs.reshape(rows_here, head_count, head_dim)
    through = jnp.cumsum(log_decay, axis=0)
    shard_fading_rates = jnp.exp(through[-1])
    incoming = carried_in(shard_fading_rates, device_state, initial_state)
    query_float = queries.reshape(rows_here, head_count, head_dim).astype(jnp.float32)
    inherited = jnp.exp(through)[:, :, None] * jnp.einsum(
        "thd,hde->the", query_float, incoming, precision=HIGH
    )
    attended = local_out + inherited
    hidden = normalize(attended, norm_gain, gate_logits)
    seq_len, tensor_len = (lax.axis_size("seq"), lax.axis_size("tensor"))
    col_blocks = seq_len // tensor_len
    route = []
    for s in range(seq_len):
        for t in range(tensor_len):
            source = (col_blocks * t + s // tensor_len) * tensor_len + s % tensor_len
            route.append((source, s * tensor_len + t))
    placed = lax.ppermute(out_weight, ("seq", "tensor"), route)
    columns = lax.all_gather(placed, "seq", axis=0, tiled=True)
    columns = columns.reshape(col_blocks, -1, columns.shape[1])
    full_hidden = lax.all_gather(hidden, "tensor", axis=1, tiled=True)
    mixed = jnp.einsum("tk,rkc->trc", full_hidden, columns, preferred_element_type=jnp.float32)
    mixed = mixed.reshape(rows_here, -1)
    return mixed


def solution(mesh):
    return jax.shard_map(
        per_device,
        mesh=mesh,
        in_specs=(
            P("seq", "tensor"),
            P("seq", "tensor"),
            P("seq", "tensor"),
            P("seq", "tensor"),
            P("seq", "tensor"),
            P("tensor", None, None),
            P("tensor"),
            P("tensor", "seq"),
        ),
        out_specs=P("seq", "tensor"),
        check_vma=False,
    )
```

profile of v0, /device:TPU:8, one launch (start us, length us, event | category | flops | bytes accessed | tf_op | source)
XLA Modules:
  0.0 229.9 jit_solution(4857555923900355773)
XLA Ops:
  6.5 0.8 copy.36
  7.4 0.2 reduce_window_sum.13
  7.7 1.1 copy.54
  8.8 1.4 fusion.4
  10.2 0.3 copy.91
  10.6 1.9 collective-permute-start
  12.5 1.4 copy.92
  13.9 9.3 %collective-permute-done = f32[8,16512]{1,0:T(8,128)S(1)} collective-permute-done((f32[8,16512]{1,0:T(8,128)S(1)}, f32[8,16512]{1,0:T(8,128)S(1)}, u32[]{:S(2)}, u32[]{:S(2)}) %collective-permute-start) | collective-permute-done | bytes 528416 | tf_op jit(solution)/shard_map/ppermute | solution.py:77
  23.3 1.9 collective-permute-start.1
  25.4 10.6 %collective-permute-done.1 = f32[8,16512]{1,0:T(8,128)S(1)} collective-permute-done((f32[8,16512]{1,0:T(8,128)S(1)}, f32[8,16512]{1,0:T(8,128)S(1)}, u32[]{:S(2)}, u32[]{:S(2)}) %collective-permute-start.1) | collective-permute-done | bytes 528416 | tf_op jit(solution)/shard_map/ppermute | solution.py:82
  36.0 0.1 slice_add_fusion.3
  36.2 1.9 collective-permute-start.2
  38.1 2.4 %collective-permute-start.6 = (bf16[1024,192]{0,1:T(8,128)(2,1)}, bf16[1024,192]{0,1:T(8,128)(2,1)S(1)}, u32[]{:S(2)}, u32[]{:S(2)}) collective-permute-start(bf16[1024,192]{0,1:T(8,128)(2,1)} %param.15), channel_id=1, source_target_pairs={{0,0},{32,1},{64,2},{96,3},{128,4},{160,5},{192,6},{224,7},{1,8},{... | collective-permute-start | bytes 1179656 | tf_op jit(solution)/shard_map/ppermute | solution.py:125
  40.5 39.4 %collective-permute-done.6 = bf16[1024,192]{0,1:T(8,128)(2,1)S(1)} collective-permute-done((bf16[1024,192]{0,1:T(8,128)(2,1)}, bf16[1024,192]{0,1:T(8,128)(2,1)S(1)}, u32[]{:S(2)}, u32[]{:S(2)}) %collective-permute-start.6) | collective-permute-done | bytes 393248 | tf_op jit(solution)/shard_map/ppermute | solution.py:125
  79.8 0.7 copy-done.2
  81.0 1.9 collective-permute-start.3
  83.0 15.8 %collective-permute-done.3 = f32[8,16512]{1,0:T(8,128)S(1)} collective-permute-done((f32[8,16512]{1,0:T(8,128)S(1)}, f32[8,16512]{1,0:T(8,128)S(1)}, u32[]{:S(2)}, u32[]{:S(2)}) %collective-permute-start.3) | collective-permute-done | bytes 528416 | tf_op jit(solution)/shard_map/ppermute | solution.py:82
  98.8 0.1 slice_add_fusion.1
  99.1 1.9 collective-permute-start.4
  101.1 20.9 %collective-permute-done.4 = f32[8,16512]{1,0:T(8,128)S(1)} collective-permute-done((f32[8,16512]{1,0:T(8,128)S(1)}, f32[8,16512]{1,0:T(8,128)S(1)}, u32[]{:S(2)}, u32[]{:S(2)}) %collective-permute-start.4) | collective-permute-done | bytes 528416 | tf_op jit(solution)/shard_map/ppermute | solution.py:82
  122.2 1.3 collective-permute-start.5
  123.7 0.7 fusion.2
  124.5 10.8 %collective-permute-done.5 = f32[8,16512]{1,0:T(8,128)S(1)} collective-permute-done((f32[8,16512]{1,0:T(8,128)S(1)}, f32[8,16512]{1,0:T(8,128)S(1)}, u32[]{:S(2)}, u32[]{:S(2)}) %collective-permute-start.5) | collective-permute-done | bytes 528416 | tf_op jit(solution)/shard_map/ppermute | solution.py:82
  135.5 0.6 fusion.3
  136.1 0.5 multiply_reduce_fusion
  136.7 0.2 copy.50
  136.9 0.9 multiply_convert_fusion
  137.8 32.2 %all-gather.5.cloned.1.call-done = bf16[32768,192]{0,1:T(8,128)(2,1)} async-done(((bf16[1024,192]{0,1:T(8,128)(2,1)}), bf16[32768,192]{0,1:T(8,128)(2,1)}) %all-gather.5.cloned.1.call-update) | async-done | bytes 12582928 | tf_op jit(solution)/shard_map/all_gather | solution.py:126
  170.1 21.3 %reshape.82 = bf16[4,8192,192]{1,0,2:T(4,128)(2,1)} reshape(bf16[32768,192]{0,1:T(8,128)(2,1)} %all-gather.5.cloned.1.call-done) | data formatting | bytes 25165824 | tf_op jit(solution)/shard_map/reshape | solution.py:127
  191.4 14.5 %copy.51 = bf16[4,192,8192]{2,1,0:T(8,128)(2,1)} copy(bf16[4,192,8192]{2,0,1:T(4,128)(2,1)} %bitcast.80) | data formatting | bytes 25165824 | tf_op jit(solution)/shard_map/tk,rkc->trc/dot_general | solution.py:129
  205.9 6.9 %all-gather.3.cloned.1.call-done = bf16[128,8192]{1,0:T(8,128)(2,1)} async-done(((bf16[128,1024]{1,0:T(8,128)(2,1)}), bf16[128,8192]{1,0:T(8,128)(2,1)}) %all-gather.3.cloned.1.call-update) | async-done | bytes 2097168 | tf_op jit(solution)/shard_map/all_gather | solution.py:128
  212.8 10.2 %fusion.41 = f32[128,768]{1,0:T(8,128)} fusion(bf16[128,8192]{1,0:T(8,128)(2,1)} %all-gather.3.cloned.1.call-done, bf16[768,8192]{1,0:T(8,128)(2,1)} %bitcast.79), kind=kOutput, calls=%fused_computation.78 | convolution fusion | flops 1610612736 | bytes 15073280 | tf_op jit(solution)/shard_map/tk,rkc->trc/dot_general | solution.py:129
  (44 shorter events, 1.9 us)
Async XLA Ops:
  6.5 117.2 %copy-start = (bf16[128,1024]{1,0:T(8,128)(2,1)S(1)}, bf16[128,1024]{1,0:T(8,128)(2,1)}, u32[]{:S(2)}) copy-start(bf16[128,1024]{1,0:T(8,128)(2,1)} %param.8) | copy-start | bytes 786436
  6.5 163.5 %all-gather.5.cloned.1.call-start = ((), (), s32[]{:S(2)}) async-start(), calls=%async_computation.1 | async-start | bytes 12976128 | tf_op jit(solution)/shard_map/all_gather | solution.py:126
  7.5 128.6 %copy-start.1 = (bf16[128,1024]{1,0:T(8,128)(2,1)S(1)}, bf16[128,1024]{1,0:T(8,128)(2,1)}, u32[]{:S(2)}) copy-start(bf16[128,1024]{1,0:T(8,128)(2,1)} %param.10) | copy-start | bytes 786436
  10.6 12.7 %collective-permute-start = (f32[8,16512]{1,0:T(8,128)S(1)}, f32[8,16512]{1,0:T(8,128)S(1)}, u32[]{:S(2)}, u32[]{:S(2)}) collective-permute-start(f32[8,16512]{1,0:T(8,128)S(1)} %pad_maximum_fusion), channel_id=1, source_target_pairs={{0,8},{8,16},{16,24},{24,32},{32,40},{40,48},{48,56},{56,64},{64,7... | collective-permute-start | bytes 1585160 | tf_op jit(solution)/shard_map/ppermute | solution.py:77
  12.5 124.4 %copy-start.3 = (bf16[128,1024]{1,0:T(8,128)(2,1)S(1)}, bf16[128,1024]{1,0:T(8,128)(2,1)}, u32[]{:S(2)}) copy-start(bf16[128,1024]{1,0:T(8,128)(2,1)} %param.11) | copy-start | bytes 786436
  12.5 124.4 %copy-start.4 = (f32[1024]{0:T(1024)S(1)}, f32[1024]{0:T(1024)}, u32[]{:S(2)}) copy-start(f32[1024]{0:T(1024)} %param.14) | copy-start | bytes 12292
  23.3 12.7 %collective-permute-start.1 = (f32[8,16512]{1,0:T(8,128)S(1)}, f32[8,16512]{1,0:T(8,128)S(1)}, u32[]{:S(2)}, u32[]{:S(2)}) collective-permute-start(f32[8,16512]{1,0:T(8,128)S(1)} %pad_select_fusion), channel_id=1, source_target_pairs={{0,8},{8,16},{16,24},{24,32},{32,40},{40,48},{48,56},{56,64},{64,7... | collective-permute-start | bytes 1585160 | tf_op jit(solution)/shard_map/ppermute | solution.py:82
  36.2 44.6 %collective-permute-start.2 = (f32[8,16512]{1,0:T(8,128)S(1)}, f32[8,16512]{1,0:T(8,128)S(1)}, u32[]{:S(2)}, u32[]{:S(2)}) collective-permute-start(f32[8,16512]{1,0:T(8,128)S(1)} %maximum_select_fusion), channel_id=1, source_target_pairs={{0,16},{8,24},{16,32},{24,40},{32,48},{40,56},{48,64},{56,72},{64,... | collective-permute-start | bytes 1585160 | tf_op jit(solution)/shard_map/ppermute | solution.py:82
  38.1 41.7 %collective-permute-start.6 = (bf16[1024,192]{0,1:T(8,128)(2,1)}, bf16[1024,192]{0,1:T(8,128)(2,1)S(1)}, u32[]{:S(2)}, u32[]{:S(2)}) collective-permute-start(bf16[1024,192]{0,1:T(8,128)(2,1)} %param.15), channel_id=1, source_target_pairs={{0,0},{32,1},{64,2},{96,3},{128,4},{160,5},{192,6},{224,7},{1,8},{... | collective-permute-start | bytes 1179656 | tf_op jit(solution)/shard_map/ppermute | solution.py:125
  79.8 0.7 copy-start.2
  80.6 132.2 %all-gather.3.cloned.1.call-start = ((), (), s32[]{:S(2)}) async-start(), calls=%async_computation | async-start | bytes 2359296 | tf_op jit(solution)/shard_map/all_gather | solution.py:128
  81.0 17.9 %collective-permute-start.3 = (f32[8,16512]{1,0:T(8,128)S(1)}, f32[8,16512]{1,0:T(8,128)S(1)}, u32[]{:S(2)}, u32[]{:S(2)}) collective-permute-start(f32[8,16512]{1,0:T(8,128)S(1)} %maximum_select_fusion.1), channel_id=1, source_target_pairs={{0,32},{8,40},{16,48},{24,56},{32,64},{40,72},{48,80},{56,88},{64,... | collective-permute-start | bytes 1585160 | tf_op jit(solution)/shard_map/ppermute | solution.py:82
  99.1 22.9 %collective-permute-start.4 = (f32[8,16512]{1,0:T(8,128)S(1)}, f32[8,16512]{1,0:T(8,128)S(1)}, u32[]{:S(2)}, u32[]{:S(2)}) collective-permute-start(f32[8,16512]{1,0:T(8,128)S(1)} %maximum_select_fusion.2), channel_id=1, source_target_pairs={{0,64},{8,72},{16,80},{24,88},{32,96},{40,104},{48,112},{56,120},{... | collective-permute-start | bytes 1585160 | tf_op jit(solution)/shard_map/ppermute | solution.py:82
  122.2 13.1 %collective-permute-start.5 = (f32[8,16512]{1,0:T(8,128)S(1)}, f32[8,16512]{1,0:T(8,128)S(1)}, u32[]{:S(2)}, u32[]{:S(2)}) collective-permute-start(f32[8,16512]{1,0:T(8,128)S(1)} %maximum_select_fusion.3), channel_id=1, source_target_pairs={{0,128},{8,136},{16,144},{24,152},{32,160},{40,168},{48,176},{56,1... | collective-permute-start | bytes 1585160 | tf_op jit(solution)/shard_map/ppermute | solution.py:82
Sparse Core Ops, SparseCore 0:
  80.7 89.2 all-gather.4
  171.8 40.9 all-gather.2
where the time goes:
time: 231 us; the launch traced here: 230 us
  waiting for transfers between devices  146 us (63%)
  local copies, waits for them, and re-layouts  41.3 us (18%)
  between operations  13.7 us (6%)
  matrix products  13.4 us (6%)
  starting transfers between devices  13.3 us (6%)
    ppermute x5, waiting for transfers between devices, carried_in(): lax.ppermute(current, 'seq', [(i, i + step) for i in range(length - step)])  58.1 us
    ppermute x1, waiting for transfers between devices, per_device(): placed = lax.ppermute(out_weight, ('seq', 'tensor'), route)  39.4 us
    all_gather x1, waiting for transfers between devices, per_device(): columns = lax.all_gather(placed, 'seq', axis=0, tiled=True)  32.2 us
    reshape x1, local copies, waits for them, and re-layouts, per_device(): columns = columns.reshape(col_blocks, -1, columns.shape[1])  21.3 us
    dot_general x1, local copies, waits for them, and re-layouts, per_device(): jnp.einsum('tk,rkc->trc', full_hidden, columns, preferred_element_type=jn...  14.5 us
    dot_general x1, matrix products, per_device(): jnp.einsum('tk,rkc->trc', full_hidden, columns, preferred_element_type=jn...  10.2 us
    ppermute x1, waiting for transfers between devices, carried_in(): shifted = lax.ppermute(own, 'seq', [(i, i + 1) for i in range(length - 1)])  9.3 us
    ppermute x5, starting transfers between devices, carried_in(): lax.ppermute(current, 'seq', [(i, i + step) for i in range(length - step)])  9 us
  transfers between devices with their start and end apart: 9, of which 8 were waited for; matrix products, arithmetic and copies ran while one was open for 18% of the time, Pallas kernels for 0%

commit v1 on v0

--- a/solution.py
+++ b/solution.py
@@ -4,6 +4,18 @@
 from jax.sharding import PartitionSpec as P
 
 HIGH = lax.Precision.HIGHEST
+
+
+def ring_product(x, axis, dim, product):
+    size, mine = (lax.axis_size(axis), lax.axis_index(axis))
+    downward = [(i, (i - 1) % size) for i in range(size)]
+    extent = x.shape[dim]
+    block = x
+    running = product(block, mine * extent)
+    for turn in range(1, size):
+        block = lax.ppermute(block, axis, downward)
+        running = running + product(block, (mine + turn) % size * extent)
+    return running
 
 
 def entering(array, axis, combine, identity):
@@ -125,8 +137,17 @@
     placed = lax.ppermute(out_weight, ("seq", "tensor"), route)
     columns = lax.all_gather(placed, "seq", axis=0, tiled=True)
     columns = columns.reshape(col_blocks, -1, columns.shape[1])
-    full_hidden = lax.all_gather(hidden, "tensor", axis=1, tiled=True)
-    mixed = jnp.einsum("tk,rkc->trc", full_hidden, columns, preferred_element_type=jnp.float32)
+    mixed = ring_product(
+        hidden,
+        "tensor",
+        1,
+        lambda part_2, at: jnp.einsum(
+            "tk,rkc->trc",
+            part_2,
+            lax.dynamic_slice_in_dim(columns, at, part_2.shape[1], axis=1),
+            preferred_element_type=jnp.float32,
+        ),
+    )
     mixed = mixed.reshape(rows_here, -1)
     return mixed
 

time: 231 us -> 252 us (1.091)
  starting transfers between devices: 13.3 us -> 47.9 us
  waiting for transfers between devices: 146 us -> 139 us
  matrix products: 13.4 us -> 7.81 us
  local copies, waits for them, and re-layouts: 41.3 us -> 38.7 us
    ppermute x0 -> x7, starting transfers between devices: none -> 34.6 us  [ring_product(): block = lax.ppermute(block, axis, downward)]
    all_gather x1, waiting for transfers between devices: 32.2 us -> 0.01 us  [per_device(): columns = lax.all_gather(placed, 'seq', axis=0, tiled=True)]
    ppermute x0 -> x7, waiting for transfers between devices: none -> 31.7 us  [ring_product(): block = lax.ppermute(block, axis, downward)]
    dot_general x1 -> x0, local copies, waits for them, and re-layouts: 14.5 us -> none  [per_device(): jnp.einsum('tk,rkc->trc', full_hidden, columns, preferred_element_type=jn...]
    dot_general x1 -> x0, matrix products: 10.2 us -> none  [per_device(): jnp.einsum('tk,rkc->trc', full_hidden, columns, preferred_element_type=jn...]
    dynamic_slice x0 -> x1, local copies, waits for them, and re-layouts: none -> 7.49 us  [per_device(): lax.dynamic_slice_in_dim(columns, at, part_2.shape[1], axis=1)]
    all_gather x1 -> x0, waiting for transfers between devices: 6.95 us -> none  [per_device(): full_hidden = lax.all_gather(hidden, 'tensor', axis=1, tiled=True)]
    unnamed x0 -> x8, matrix products: none -> 4.61 us
  transfers between devices with their start and end apart: 9 -> 15, of which waited for: 8 -> 12; matrix products, arithmetic and copies ran while one was open for 18% -> 16% of each run, Pallas kernels for 0% -> 0%
where the time goes in v1:
time: 252 us; the launch traced here: 249 us
  waiting for transfers between devices  139 us (55%)
  starting transfers between devices  47.9 us (19%)
  local copies, waits for them, and re-layouts  38.7 us (15%)
  between operations  13.8 us (5%)
  matrix products  7.81 us (3%)
    ppermute x5, waiting for transfers between devices, carried_in(): lax.ppermute(current, 'seq', [(i, i + step) for i in range(length - step)])  58.1 us
    ppermute x1, waiting for transfers between devices, per_device(): placed = lax.ppermute(out_weight, ('seq', 'tensor'), route)  39 us
    ppermute x7, starting transfers between devices, ring_product(): block = lax.ppermute(block, axis, downward)  34.6 us
    ppermute x7, waiting for transfers between devices, ring_product(): block = lax.ppermute(block, axis, downward)  31.7 us
    reshape x1, local copies, waits for them, and re-layouts, per_device(): columns = columns.reshape(col_blocks, -1, columns.shape[1])  21.3 us
    ppermute x1, waiting for transfers between devices, carried_in(): shifted = lax.ppermute(own, 'seq', [(i, i + 1) for i in range(length - 1)])  10.4 us
    ppermute x5, starting transfers between devices, carried_in(): lax.ppermute(current, 'seq', [(i, i + step) for i in range(length - step)])  9.01 us
    dynamic_slice x1, local copies, waits for them, and re-layouts, per_device(): lax.dynamic_slice_in_dim(columns, at, part_2.shape[1], axis=1)  7.49 us
  transfers between devices with their start and end apart: 15, of which 12 were waited for; matrix products, arithmetic and copies ran while one was open for 16% of the time, Pallas kernels for 0%

profile of v1, /device:TPU:8, one launch (start us, length us, event | category | flops | bytes accessed | tf_op | source)
XLA Modules:
  0.0 249.2 jit_solution(13869286828896277173)
XLA Ops:
  6.5 0.8 copy.46
  7.6 1.1 copy.80
  8.8 1.4 fusion.4
  10.6 1.9 collective-permute-start
  12.9 10.4 %collective-permute-done = f32[8,16512]{1,0:T(8,128)S(1)} collective-permute-done((f32[8,16512]{1,0:T(8,128)S(1)}, f32[8,16512]{1,0:T(8,128)S(1)}, u32[]{:S(2)}, u32[]{:S(2)}) %collective-permute-start) | collective-permute-done | bytes 528416 | tf_op jit(solution)/shard_map/ppermute | solution.py:89
  23.4 1.9 collective-permute-start.1
  25.4 10.6 %collective-permute-done.1 = f32[8,16512]{1,0:T(8,128)S(1)} collective-permute-done((f32[8,16512]{1,0:T(8,128)S(1)}, f32[8,16512]{1,0:T(8,128)S(1)}, u32[]{:S(2)}, u32[]{:S(2)}) %collective-permute-start.1) | collective-permute-done | bytes 528416 | tf_op jit(solution)/shard_map/ppermute | solution.py:94
  36.2 1.9 collective-permute-start.2
  38.2 2.4 collective-permute-start.6
  40.5 39.0 %collective-permute-done.6 = bf16[1024,192]{0,1:T(8,128)(2,1)S(1)} collective-permute-done((bf16[1024,192]{0,1:T(8,128)(2,1)S(1)}, bf16[1024,192]{0,1:T(8,128)(2,1)S(1)}, u32[]{:S(2)}, u32[]{:S(2)}) %collective-permute-start.6) | collective-permute-done | bytes 393248 | tf_op jit(solution)/shard_map/ppermute | solution.py:137
  79.6 0.7 copy-done.4
  80.7 1.9 collective-permute-start.3
  82.7 15.8 %collective-permute-done.3 = f32[8,16512]{1,0:T(8,128)S(1)} collective-permute-done((f32[8,16512]{1,0:T(8,128)S(1)}, f32[8,16512]{1,0:T(8,128)S(1)}, u32[]{:S(2)}, u32[]{:S(2)}) %collective-permute-start.3) | collective-permute-done | bytes 528416 | tf_op jit(solution)/shard_map/ppermute | solution.py:94
  98.7 1.9 collective-permute-start.4
  100.8 20.9 %collective-permute-done.4 = f32[8,16512]{1,0:T(8,128)S(1)} collective-permute-done((f32[8,16512]{1,0:T(8,128)S(1)}, f32[8,16512]{1,0:T(8,128)S(1)}, u32[]{:S(2)}, u32[]{:S(2)}) %collective-permute-start.4) | collective-permute-done | bytes 528416 | tf_op jit(solution)/shard_map/ppermute | solution.py:94
  121.9 1.3 collective-permute-start.5
  124.1 10.8 %collective-permute-done.5 = f32[8,16512]{1,0:T(8,128)S(1)} collective-permute-done((f32[8,16512]{1,0:T(8,128)S(1)}, f32[8,16512]{1,0:T(8,128)S(1)}, u32[]{:S(2)}, u32[]{:S(2)}) %collective-permute-start.5) | collective-permute-done | bytes 528416 | tf_op jit(solution)/shard_map/ppermute | solution.py:94
  137.8 7.7 %collective-permute-done.7 = bf16[128,1024]{1,0:T(8,128)(2,1)S(1)} collective-permute-done((bf16[128,1024]{1,0:T(8,128)(2,1)S(1)}, bf16[128,1024]{1,0:T(8,128)(2,1)S(1)}, u32[]{:S(2)}, u32[]{:S(2)}) %collective-permute-start.7) | collective-permute-done | bytes 262176 | tf_op jit(solution)/shard_map/ppermute | solution.py:16
  145.5 16.1 %collective-permute-start.8 = (bf16[128,1024]{1,0:T(8,128)(2,1)S(1)}, bf16[128,1024]{1,0:T(8,128)(2,1)S(1)}, u32[]{:S(2)}, u32[]{:S(2)}) collective-permute-start(bf16[128,1024]{1,0:T(8,128)(2,1)S(1)} %collective-permute-done.7), channel_id=1, source_target_pairs={{0,7},{1,0},{2,1},{3,2},{4,3},{5,4},{6,5},{7,6},{8,15},{9,8},{10,9... | collective-permute-start | bytes 786440 | tf_op jit(solution)/shard_map/ppermute | solution.py:16
  161.6 6.3 %collective-permute-done.8 = bf16[128,1024]{1,0:T(8,128)(2,1)S(1)} collective-permute-done((bf16[128,1024]{1,0:T(8,128)(2,1)S(1)}, bf16[128,1024]{1,0:T(8,128)(2,1)S(1)}, u32[]{:S(2)}, u32[]{:S(2)}) %collective-permute-start.8) | collective-permute-done | bytes 262176 | tf_op jit(solution)/shard_map/ppermute | solution.py:16
  167.8 3.7 %collective-permute-start.9 = (bf16[128,1024]{1,0:T(8,128)(2,1)S(1)}, bf16[128,1024]{1,0:T(8,128)(2,1)S(1)}, u32[]{:S(2)}, u32[]{:S(2)}) collective-permute-start(bf16[128,1024]{1,0:T(8,128)(2,1)S(1)} %collective-permute-done.8), channel_id=1, source_target_pairs={{0,7},{1,0},{2,1},{3,2},{4,3},{5,4},{6,5},{7,6},{8,15},{9,8},{10,9... | collective-permute-start | bytes 786440 | tf_op jit(solution)/shard_map/ppermute | solution.py:16
  171.5 5.4 %collective-permute-done.9 = bf16[128,1024]{1,0:T(8,128)(2,1)S(1)} collective-permute-done((bf16[128,1024]{1,0:T(8,128)(2,1)S(1)}, bf16[128,1024]{1,0:T(8,128)(2,1)S(1)}, u32[]{:S(2)}, u32[]{:S(2)}) %collective-permute-start.9) | collective-permute-done | bytes 262176 | tf_op jit(solution)/shard_map/ppermute | solution.py:16
  176.9 3.7 %collective-permute-start.10 = (bf16[128,1024]{1,0:T(8,128)(2,1)S(1)}, bf16[128,1024]{1,0:T(8,128)(2,1)S(1)}, u32[]{:S(2)}, u32[]{:S(2)}) collective-permute-start(bf16[128,1024]{1,0:T(8,128)(2,1)S(1)} %collective-permute-done.9), channel_id=1, source_target_pairs={{0,7},{1,0},{2,1},{3,2},{4,3},{5,4},{6,5},{7,6},{8,15},{9,8},{10,9... | collective-permute-start | bytes 786440 | tf_op jit(solution)/shard_map/ppermute | solution.py:16
  180.6 4.5 %collective-permute-done.10 = bf16[128,1024]{1,0:T(8,128)(2,1)S(1)} collective-permute-done((bf16[128,1024]{1,0:T(8,128)(2,1)S(1)}, bf16[128,1024]{1,0:T(8,128)(2,1)S(1)}, u32[]{:S(2)}, u32[]{:S(2)}) %collective-permute-start.10) | collective-permute-done | bytes 262176 | tf_op jit(solution)/shard_map/ppermute | solution.py:16
  185.2 3.7 %collective-permute-start.11 = (bf16[128,1024]{1,0:T(8,128)(2,1)S(1)}, bf16[128,1024]{1,0:T(8,128)(2,1)S(1)}, u32[]{:S(2)}, u32[]{:S(2)}) collective-permute-start(bf16[128,1024]{1,0:T(8,128)(2,1)S(1)} %collective-permute-done.10), channel_id=1, source_target_pairs={{0,7},{1,0},{2,1},{3,2},{4,3},{5,4},{6,5},{7,6},{8,15},{9,8},{10,9... | collective-permute-start | bytes 786440 | tf_op jit(solution)/shard_map/ppermute | solution.py:16
  188.9 3.9 %collective-permute-done.11 = bf16[128,1024]{1,0:T(8,128)(2,1)S(1)} collective-permute-done((bf16[128,1024]{1,0:T(8,128)(2,1)S(1)}, bf16[128,1024]{1,0:T(8,128)(2,1)S(1)}, u32[]{:S(2)}, u32[]{:S(2)}) %collective-permute-start.11) | collective-permute-done | bytes 262176 | tf_op jit(solution)/shard_map/ppermute | solution.py:16
  192.7 3.7 %collective-permute-start.12 = (bf16[128,1024]{1,0:T(8,128)(2,1)S(1)}, bf16[128,1024]{1,0:T(8,128)(2,1)S(1)}, u32[]{:S(2)}, u32[]{:S(2)}) collective-permute-start(bf16[128,1024]{1,0:T(8,128)(2,1)S(1)} %collective-permute-done.11), channel_id=1, source_target_pairs={{0,7},{1,0},{2,1},{3,2},{4,3},{5,4},{6,5},{7,6},{8,15},{9,8},{10,9... | collective-permute-start | bytes 786440 | tf_op jit(solution)/shard_map/ppermute | solution.py:16
  196.4 3.9 %collective-permute-done.12 = bf16[128,1024]{1,0:T(8,128)(2,1)S(1)} collective-permute-done((bf16[128,1024]{1,0:T(8,128)(2,1)S(1)}, bf16[128,1024]{1,0:T(8,128)(2,1)S(1)}, u32[]{:S(2)}, u32[]{:S(2)}) %collective-permute-start.12) | collective-permute-done | bytes 262176 | tf_op jit(solution)/shard_map/ppermute | solution.py:16
  200.3 3.7 %collective-permute-start.13 = (bf16[128,1024]{1,0:T(8,128)(2,1)S(1)}, bf16[128,1024]{1,0:T(8,128)(2,1)S(1)}, u32[]{:S(2)}, u32[]{:S(2)}) collective-permute-start(bf16[128,1024]{1,0:T(8,128)(2,1)S(1)} %collective-permute-done.12), channel_id=1, source_target_pairs={{0,7},{1,0},{2,1},{3,2},{4,3},{5,4},{6,5},{7,6},{8,15},{9,8},{10,9... | collective-permute-start | bytes 786440 | tf_op jit(solution)/shard_map/ppermute | solution.py:16
  204.0 21.3 %reshape.83 = bf16[4,8192,192]{1,0,2:T(4,128)(2,1)} reshape(bf16[32768,192]{0,1:T(8,128)(2,1)} %all-gather.2.cloned.1.call-done) | data formatting | bytes 25165824 | tf_op jit(solution)/shard_map/reshape | solution.py:139
  225.3 7.5 %constant_dynamic-slice_fusion.6 = (bf16[4,1024,192]{1,0,2:T(4,128)(2,1)S(1)}, bf16[4,1024,192]{1,0,2:T(4,128)(2,1)S(1)}, bf16[4,1024,192]{1,0,2:T(4,128)(2,1)S(...) fusion(bf16[4,8192,192]{1,0,2:T(4,128)(2,1)} %reshape.83, ...), kind=kLoop, calls=%fused_computation.79 | loop fusion | bytes 25165856 | tf_op jit(solution)/shard_map/dynamic_slice | solution.py:147
  241.4 0.9 copy.69
  (78 shorter events, 14.5 us)
Async XLA Ops:
  6.5 116.8 %copy-start = (bf16[128,1024]{1,0:T(8,128)(2,1)S(1)}, bf16[128,1024]{1,0:T(8,128)(2,1)}, u32[]{:S(2)}) copy-start(bf16[128,1024]{1,0:T(8,128)(2,1)} %param.8) | copy-start | bytes 786436
  6.5 197.5 %all-gather.2.cloned.1.call-start = ((), (), s32[]{:S(2)}) async-start(), calls=%async_computation | async-start | bytes 12976128 | tf_op jit(solution)/shard_map/all_gather | solution.py:138
  8.8 3.8 %copy-start.3 = (f32[8,128,128]{2,1,0:T(8,128)S(1)}, f32[8,128,128]{2,1,0:T(8,128)}, u32[]{:S(2)}) copy-start(f32[8,128,128]{2,1,0:T(8,128)} %param.13) | copy-start | bytes 1572868
  10.6 12.7 %collective-permute-start = (f32[8,16512]{1,0:T(8,128)S(1)}, f32[8,16512]{1,0:T(8,128)S(1)}, u32[]{:S(2)}, u32[]{:S(2)}) collective-permute-start(f32[8,16512]{1,0:T(8,128)S(1)} %pad_maximum_fusion), channel_id=1, source_target_pairs={{0,8},{8,16},{16,24},{24,32},{32,40},{40,48},{48,56},{56,64},{64,7... | collective-permute-start | bytes 1585160 | tf_op jit(solution)/shard_map/ppermute | solution.py:89
  23.4 12.7 %collective-permute-start.1 = (f32[8,16512]{1,0:T(8,128)S(1)}, f32[8,16512]{1,0:T(8,128)S(1)}, u32[]{:S(2)}, u32[]{:S(2)}) collective-permute-start(f32[8,16512]{1,0:T(8,128)S(1)} %pad_select_fusion), channel_id=1, source_target_pairs={{0,8},{8,16},{16,24},{24,32},{32,40},{40,48},{48,56},{56,64},{64,7... | collective-permute-start | bytes 1585160 | tf_op jit(solution)/shard_map/ppermute | solution.py:94
  36.0 2.1 copy-start.7
  36.2 44.2 %collective-permute-start.2 = (f32[8,16512]{1,0:T(8,128)S(1)}, f32[8,16512]{1,0:T(8,128)S(1)}, u32[]{:S(2)}, u32[]{:S(2)}) collective-permute-start(f32[8,16512]{1,0:T(8,128)S(1)} %maximum_select_fusion), channel_id=1, source_target_pairs={{0,16},{8,24},{16,32},{24,40},{32,48},{40,56},{48,64},{56,72},{64,... | collective-permute-start | bytes 1585160 | tf_op jit(solution)/shard_map/ppermute | solution.py:94
  38.2 41.4 %collective-permute-start.6 = (bf16[1024,192]{0,1:T(8,128)(2,1)S(1)}, bf16[1024,192]{0,1:T(8,128)(2,1)S(1)}, u32[]{:S(2)}, u32[]{:S(2)}) collective-permute-start(bf16[1024,192]{0,1:T(8,128)(2,1)S(1)} %copy-done.7), channel_id=1, source_target_pairs={{0,0},{32,1},{64,2},{96,3},{128,4},{160,5},{192,6},{224,7},{1,8},{... | collective-permute-start | bytes 1179656 | tf_op jit(solution)/shard_map/ppermute | solution.py:137
  79.6 0.7 copy-start.4
  80.7 17.9 %collective-permute-start.3 = (f32[8,16512]{1,0:T(8,128)S(1)}, f32[8,16512]{1,0:T(8,128)S(1)}, u32[]{:S(2)}, u32[]{:S(2)}) collective-permute-start(f32[8,16512]{1,0:T(8,128)S(1)} %maximum_select_fusion.1), channel_id=1, source_target_pairs={{0,32},{8,40},{16,48},{24,56},{32,64},{40,72},{48,80},{56,88},{64,... | collective-permute-start | bytes 1585160 | tf_op jit(solution)/shard_map/ppermute | solution.py:94
  98.7 22.9 %collective-permute-start.4 = (f32[8,16512]{1,0:T(8,128)S(1)}, f32[8,16512]{1,0:T(8,128)S(1)}, u32[]{:S(2)}, u32[]{:S(2)}) collective-permute-start(f32[8,16512]{1,0:T(8,128)S(1)} %maximum_select_fusion.2), channel_id=1, source_target_pairs={{0,64},{8,72},{16,80},{24,88},{32,96},{40,104},{48,112},{56,120},{... | collective-permute-start | bytes 1585160 | tf_op jit(solution)/shard_map/ppermute | solution.py:94
  121.9 13.1 %collective-permute-start.5 = (f32[8,16512]{1,0:T(8,128)S(1)}, f32[8,16512]{1,0:T(8,128)S(1)}, u32[]{:S(2)}, u32[]{:S(2)}) collective-permute-start(f32[8,16512]{1,0:T(8,128)S(1)} %maximum_select_fusion.3), channel_id=1, source_target_pairs={{0,128},{8,136},{16,144},{24,152},{32,160},{40,168},{48,176},{56,1... | collective-permute-start | bytes 1585160 | tf_op jit(solution)/shard_map/ppermute | solution.py:94
  135.1 1.0 copy-start.2
  136.6 1.0 copy-start.5
  136.6 0.9 copy-start.6
  137.7 7.8 %collective-permute-start.7 = (bf16[128,1024]{1,0:T(8,128)(2,1)S(1)}, bf16[128,1024]{1,0:T(8,128)(2,1)S(1)}, u32[]{:S(2)}, u32[]{:S(2)}) collective-permute-start(bf16[128,1024]{1,0:T(8,128)(2,1)S(1)} %multiply_convert_fusion), channel_id=1, source_target_pairs={{0,7},{1,0},{2,1},{3,2},{4,3},{5,4},{6,5},{7,6},{8,15},{9,8},{10,9... | collective-permute-start | bytes 786440 | tf_op jit(solution)/shard_map/ppermute | solution.py:16
  145.5 22.3 %collective-permute-start.8 = (bf16[128,1024]{1,0:T(8,128)(2,1)S(1)}, bf16[128,1024]{1,0:T(8,128)(2,1)S(1)}, u32[]{:S(2)}, u32[]{:S(2)}) collective-permute-start(bf16[128,1024]{1,0:T(8,128)(2,1)S(1)} %collective-permute-done.7), channel_id=1, source_target_pairs={{0,7},{1,0},{2,1},{3,2},{4,3},{5,4},{6,5},{7,6},{8,15},{9,8},{10,9... | collective-permute-start | bytes 786440 | tf_op jit(solution)/shard_map/ppermute | solution.py:16
  167.8 9.1 %collective-permute-start.9 = (bf16[128,1024]{1,0:T(8,128)(2,1)S(1)}, bf16[128,1024]{1,0:T(8,128)(2,1)S(1)}, u32[]{:S(2)}, u32[]{:S(2)}) collective-permute-start(bf16[128,1024]{1,0:T(8,128)(2,1)S(1)} %collective-permute-done.8), channel_id=1, source_target_pairs={{0,7},{1,0},{2,1},{3,2},{4,3},{5,4},{6,5},{7,6},{8,15},{9,8},{10,9... | collective-permute-start | bytes 786440 | tf_op jit(solution)/shard_map/ppermute | solution.py:16
  176.9 8.2 %collective-permute-start.10 = (bf16[128,1024]{1,0:T(8,128)(2,1)S(1)}, bf16[128,1024]{1,0:T(8,128)(2,1)S(1)}, u32[]{:S(2)}, u32[]{:S(2)}) collective-permute-start(bf16[128,1024]{1,0:T(8,128)(2,1)S(1)} %collective-permute-done.9), channel_id=1, source_target_pairs={{0,7},{1,0},{2,1},{3,2},{4,3},{5,4},{6,5},{7,6},{8,15},{9,8},{10,9... | collective-permute-start | bytes 786440 | tf_op jit(solution)/shard_map/ppermute | solution.py:16
  185.2 7.6 %collective-permute-start.11 = (bf16[128,1024]{1,0:T(8,128)(2,1)S(1)}, bf16[128,1024]{1,0:T(8,128)(2,1)S(1)}, u32[]{:S(2)}, u32[]{:S(2)}) collective-permute-start(bf16[128,1024]{1,0:T(8,128)(2,1)S(1)} %collective-permute-done.10), channel_id=1, source_target_pairs={{0,7},{1,0},{2,1},{3,2},{4,3},{5,4},{6,5},{7,6},{8,15},{9,8},{10,9... | collective-permute-start | bytes 786440 | tf_op jit(solution)/shard_map/ppermute | solution.py:16
  192.7 7.6 %collective-permute-start.12 = (bf16[128,1024]{1,0:T(8,128)(2,1)S(1)}, bf16[128,1024]{1,0:T(8,128)(2,1)S(1)}, u32[]{:S(2)}, u32[]{:S(2)}) collective-permute-start(bf16[128,1024]{1,0:T(8,128)(2,1)S(1)} %collective-permute-done.11), channel_id=1, source_target_pairs={{0,7},{1,0},{2,1},{3,2},{4,3},{5,4},{6,5},{7,6},{8,15},{9,8},{10,9... | collective-permute-start | bytes 786440 | tf_op jit(solution)/shard_map/ppermute | solution.py:16
  200.3 40.4 %collective-permute-start.13 = (bf16[128,1024]{1,0:T(8,128)(2,1)S(1)}, bf16[128,1024]{1,0:T(8,128)(2,1)S(1)}, u32[]{:S(2)}, u32[]{:S(2)}) collective-permute-start(bf16[128,1024]{1,0:T(8,128)(2,1)S(1)} %collective-permute-done.12), channel_id=1, source_target_pairs={{0,7},{1,0},{2,1},{3,2},{4,3},{5,4},{6,5},{7,6},{8,15},{9,8},{10,9... | collective-permute-start | bytes 786440 | tf_op jit(solution)/shard_map/ppermute | solution.py:16
  241.3 1.1 copy-start.1
Sparse Core Ops, SparseCore 0:
  80.5 88.5 all-gather.1
